TPU v7x, 256 devices: a whole 4x4x8 slice. The times are simulated.
256 devices in a mesh: req: 8 (over y, core), vocab: 32 (over x, z).
Axes of the slice: x: 4, y: 4, z: 8, core: 2. Of those that a mesh axis runs over, the one named last changes fastest.
Arguments:
- hidden_rows: bfloat16 [8192, 2048], P(('req', 'vocab')), may hold values from -20 to 20
- norm_gain: float32 [2048], replicated, may hold values from 0.1 to 1.9
- head_weight: bfloat16 [2048, 81920], P(None, 'vocab'), may hold values from -10 to 10
- token_ids: int32 [8192], P('req'), may hold values from 0 to 81919
- live_count: int32 [256], P(('req', 'vocab')), may hold values from 1 to 32, as said below
Outputs:
- logprob: float32 [8192], P(('req', 'vocab'))
- entropy: float32 [8192], P(('req', 'vocab'))
Inputs may be any that keep to these rules, and one draw needn't show every extreme that they name: `live_count`: the live rows of an owner are its first ones; some owner has all 32 live in every draw.
All inputs are finite; a program needn't handle non-finite values.
Results may differ from a plain program's by a relative error of at most 0.012.
Values may be sent and summed in bfloat16 or wider, within the bound.
A program may use at most 64 MiB of HBM per device.

v0:
```python
import jax
import jax.numpy as jnp
from jax import lax
from jax.sharding import PartitionSpec as P


def local_stats(row_block, labels, columns, first_col):
    logits = jnp.dot(row_block, columns, preferred_element_type=jnp.float32)
    row_top = jnp.max(logits, axis=1)
    shifted = logits - row_top[:, None]
    powers = jnp.exp(shifted)
    row_total = jnp.sum(powers, axis=1)
    row_spread = jnp.sum(powers * shifted, axis=1)
    width = columns.shape[1]
    offset = labels - first_col
    inside = (offset >= 0) & (offset < width)
    chosen = jnp.take_along_axis(logits, jnp.clip(offset, 0, width - 1)[:, None], axis=1)[:, 0]
    row_picked = jnp.where(inside, chosen, 0.0)
    return (row_top, row_total, row_spread, row_picked)


def rescale(row_top, row_total, row_spread, global_top):
    factor = jnp.exp(row_top - global_top)
    return (row_total * factor, (row_spread + (row_top - global_top) * row_total) * factor)


def finish(global_top, row_total, row_spread, row_picked, live_count, own_rows):
    log_total = jnp.log(row_total)
    logprob = row_picked - global_top - log_total
    entropy = log_total - row_spread / row_total
    live = jnp.arange(own_rows, dtype=jnp.int32) < live_count[0]
    return (jnp.where(live, logprob, 0.0), jnp.where(live, entropy, 0.0))


def own_slice(array, start, own_rows):
    return lax.dynamic_slice_in_dim(array, start, own_rows, 0)


def per_device(hidden_rows, norm_gain, head_weight, token_ids, live_count):
    own_rows = hidden_rows.shape[0]
    shard_width = head_weight.shape[1]
    values = hidden_rows.astype(jnp.float32)
    squares = jnp.mean(values * values, axis=1)
    normed = (values * lax.rsqrt(squares + 1e-06)[:, None] * norm_gain[None, :]).astype(
        jnp.bfloat16
    )
    gathered = lax.all_gather(normed, "vocab", axis=0, tiled=True)
    first_col = lax.axis_index("vocab") * shard_width
    row_top, row_total, row_spread, row_picked = local_stats(
        gathered, token_ids, head_weight, first_col
    )
    start = lax.axis_index("vocab") * own_rows
    global_top = lax.pmax(row_top, "vocab")
    scaled_total, scaled_spread = rescale(row_top, row_total, row_spread, global_top)
    summed_total, summed_spread, summed_picked = lax.psum(
        (scaled_total, scaled_spread, row_picked), "vocab"
    )
    return finish(
        own_slice(global_top, start, own_rows),
        own_slice(summed_total, start, own_rows),
        own_slice(summed_spread, start, own_rows),
        own_slice(summed_picked, start, own_rows),
        live_count,
        own_rows,
    )


def solution(mesh):
    placed = (P(("req", "vocab"), None), P(), P(None, "vocab"), P("req"), P(("req", "vocab")))
    return jax.shard_map(
        per_device,
        mesh=mesh,
        in_specs=placed,
        out_specs=(P(("req", "vocab")), P(("req", "vocab"))),
        check_vma=False,
    )
```

profile of v0, /device:TPU:8, one launch (start us, length us, event | category | flops | bytes accessed | tf_op | source)
XLA Modules:
  0.0 353.2 jit_solution(11047198373892118158)
XLA Ops:
  7.2 0.0 all-gather.2.cloned.1.call-start
  7.2 1.0 fusion.1
  8.3 1.7 fusion.3
  9.9 0.0 all-gather.2.cloned.1.call-update
  10.6 0.7 compare_select_fusion
  11.3 83.8 %all-gather.2.cloned.1.call-done = bf16[1024,2048]{1,0:T(8,128)(2,1)} async-done(((bf16[32,2048]{1,0:T(8,128)(2,1)}), bf16[1024,2048]{1,0:T(8,128)(2,1)}) %all-gather.2.cloned.1.call-update) | async-done | bytes 4194320 | tf_op jit(solution)/shard_map/all_gather | solution.py:47
  95.2 17.6 %fusion.7 = (f32[1024]{0:T(1024)S(1)}, f32[1024,2560]{1,0:T(8,128)}) fusion(bf16[1024,2048]{1,0:T(8,128)(2,1)} %all-gather.2.cloned.1.call-done, bf16[2048,2560]{1,0:T(8,128)(2,1)} %param.7), kind=kOutput, calls=%fused_computation.22 | convolution fusion | flops 10740038656 | bytes 25169920 | tf_op jit(solution)/shard_map/dot_general | solution.py:8
  112.8 0.0 copy-start
  112.8 71.8 %pmax.7 = f32[1024]{0:T(1024)S(1)} all-reduce(f32[1024]{0:T(1024)S(1)} %get-tuple-element.11), channel_id=1, replica_groups=mesh['req'=8,'vocab'=32] {'vocab'}, use_global_device_ids=true, to_apply=%region_3.0 | all-reduce | flops 1024 | bytes 8192 | tf_op jit(solution)/shard_map/pmax | solution.py:53
  184.6 6.3 %fusion = (f32[1024]{0:T(1024)S(1)}, f32[1024]{0:T(1024)S(1)}) fusion(f32[1024,2560]{1,0:T(8,128)} %get-tuple-element.12, f32[1024]{0:T(1024)S(1)} %get-tuple-element.11), kind=kLoop, calls=%fused_computation.3 | loop fusion | flops 10483712 | bytes 10498048 | tf_op jit(solution)/shard_map/reduce_sum | solution.py:13
  190.9 17.0 %gather_fusion = f32[1024]{0:T(1024)S(1)} fusion(f32[1024,2560]{1,0:T(8,128)} %get-tuple-element.12, s32[1024]{0:T(1024)S(1)} %bitcast.8), kind=kCustom, calls=%fused_computation | custom fusion | bytes 16384 | tf_op jit(solution)/shard_map/jit(take_along_axis)/gather | solution.py:17
  208.0 0.0 copy-done
  208.0 137.7 %all-reduce = (f32[1024]{0:T(1024)S(1)}, f32[1024]{0:T(1024)S(1)}, f32[1024]{0:T(1024)S(1)}) all-reduce(f32[1024]{0:T(1024)S(1)} %select_select_fusion, f32[1024]{0:T(1024)S(1)} %get-tuple-element.8, f32[1024]{0:T(1024)S(1)} %get-tuple-element.7), channel_id=1, replica_groups=mesh['req'=8,'vocab'=32] {'vocab'}, use_global_device_ids=true, to_apply=%region_1.0 | all-reduce | flops 3072 | bytes 24576 | tf_op jit(solution)/shard_map/psum | solution.py:55
  345.8 0.6 compare_select_fusion.1
  (6 shorter events, 0.1 us)
Async XLA Ops:
  7.2 88.0 %all-gather.2.cloned.1.call-start = ((), (), s32[]{:S(2)}) async-start(), calls=%async_computation | async-start | bytes 4325376 | tf_op jit(solution)/shard_map/all_gather | solution.py:47
  112.8 95.2 %copy-start = (s32[1024]{0:T(1024)S(1)}, s32[1024]{0:T(1024)}, u32[]{:S(2)}) copy-start(s32[1024]{0:T(1024)} %param.8) | copy-start | bytes 12292
Sparse Core Ops, SparseCore 0:
  10.6 84.5 all-gather.1
where the time goes:
time: 354 us; the launch traced here: 353 us
  blocking collectives  210 us (59%)
  waiting for transfers between devices  83.9 us (24%)
  matrix products  17.6 us (5%)
  local copies, waits for them, and re-layouts  17.1 us (5%)
  between operations  14.7 us (4%)
  other arithmetic  10.4 us (3%)
    psum x1, blocking collectives, per_device(): lax.psum((scaled_total, scaled_spread, row_picked), 'vocab')  138 us
    all_gather x1, waiting for transfers between devices, per_device(): gathered = lax.all_gather(normed, 'vocab', axis=0, tiled=True)  83.8 us
    pmax x1, blocking collectives, per_device(): global_top = lax.pmax(row_top, 'vocab')  71.8 us
    dot_general x1, matrix products, local_stats(): logits = jnp.dot(row_block, columns, preferred_element_type=jnp.float32)  17.6 us
    gather x1, local copies, waits for them, and re-layouts, local_stats(): jnp.take_along_axis(logits, jnp.clip(offset, 0, width - 1)[:, None], axis=1)  17 us
  transfers between devices with their start and end apart: 1, of which 1 were waited for; matrix products, arithmetic and copies ran while one was open for 0% of the time, Pallas kernels for 0%

commit v1 on v0

--- a/solution.py
+++ b/solution.py
@@ -44,7 +44,9 @@
     normed = (values * lax.rsqrt(squares + 1e-06)[:, None] * norm_gain[None, :]).astype(
         jnp.bfloat16
     )
-    gathered = lax.all_gather(normed, "vocab", axis=0, tiled=True)
+    gathered = jnp.concatenate(
+        lax.all_to_all(jnp.stack([normed] * lax.axis_size("vocab")), "vocab", 0, 0), axis=0
+    )
     first_col = lax.axis_index("vocab") * shard_width
     row_top, row_total, row_spread, row_picked = local_stats(
         gathered, token_ids, head_weight, first_col

time: 354 us -> 366 us (1.034)
  between operations: 14.7 us -> 1.37 us
  waiting for transfers between devices: 83.9 us -> 96.3 us
  starting transfers between devices: 0.04 us -> 11.4 us
    all_to_all x0 -> x1, waiting for transfers between devices: none -> 96.3 us  [per_device(): lax.all_to_all(jnp.stack([normed] * lax.axis_size('vocab')), 'vocab', 0, 0)]
    all_gather x1 -> x0, waiting for transfers between devices: 83.8 us -> none  [per_device(): gathered = lax.all_gather(normed, 'vocab', axis=0, tiled=True)]
    all_to_all x0 -> x1, starting transfers between devices: none -> 11.4 us  [per_device(): lax.all_to_all(jnp.stack([normed] * lax.axis_size('vocab')), 'vocab', 0, 0)]
where the time goes in v1:
time: 366 us; the launch traced here: 365 us
  blocking collectives  209 us (57%)
  waiting for transfers between devices  96.3 us (26%)
  local copies, waits for them, and re-layouts  19.5 us (5%)
  matrix products  17.6 us (5%)
  starting transfers between devices  11.4 us (3%)
  other arithmetic  9.04 us (2%)
    psum x1, blocking collectives, per_device(): lax.psum((scaled_total, scaled_spread, row_picked), 'vocab')  138 us
    all_to_all x1, waiting for transfers between devices, per_device(): lax.all_to_all(jnp.stack([normed] * lax.axis_size('vocab')), 'vocab', 0, 0)  96.3 us
    pmax x1, blocking collectives, per_device(): global_top = lax.pmax(row_top, 'vocab')  71.5 us
    dot_general x1, matrix products, local_stats(): logits = jnp.dot(row_block, columns, preferred_element_type=jnp.float32)  17.6 us
    gather x1, local copies, waits for them, and re-layouts, local_stats(): jnp.take_along_axis(logits, jnp.clip(offset, 0, width - 1)[:, None], axis=1)  17 us
    all_to_all x1, starting transfers between devices, per_device(): lax.all_to_all(jnp.stack([normed] * lax.axis_size('vocab')), 'vocab', 0, 0)  11.4 us
  transfers between devices with their start and end apart: 1, of which 1 were waited for; matrix products, arithmetic and copies ran while one was open for 0% of the time, Pallas kernels for 0%

profile of v1, /device:TPU:8, one launch (start us, length us, event | category | flops | bytes accessed | tf_op | source)
XLA Modules:
  0.0 364.7 jit_solution(8060195230436993559)
XLA Ops:
  0.6 0.0 copy-start
  0.6 1.0 fusion.1
  1.7 1.0 fusion.3
  2.7 2.5 stack.2
  5.2 11.4 %all-to-all-start = ((bf16[32,32,2048]{2,1,0:T(8,128)(2,1)}), bf16[32,32,2048]{2,1,0:T(8,128)(2,1)}, u32[]{:S(2)}, u32[]{:S(2)}) async-start(bf16[32,32,2048]{2,1,0:T(8,128)(2,1)} %stack.2), calls=%async_computation | async-start | bytes 8388608 | tf_op jit(solution)/shard_map/all_to_all | solution.py:48
  17.3 0.0 copy-done
  17.3 96.3 %all-to-all-done = bf16[32,32,2048]{2,1,0:T(8,128)(2,1)} async-done(((bf16[32,32,2048]{2,1,0:T(8,128)(2,1)}), bf16[32,32,2048]{2,1,0:T(8,128)(2,1)}, u32[]{:S(2)}, u32[]{:S(2)}) %all-to-all-start) | async-done | bytes 4194336 | tf_op jit(solution)/shard_map/all_to_all | solution.py:48
  113.6 17.6 %fusion.7 = (f32[1024]{0:T(1024)S(1)}, f32[1024,2560]{1,0:T(8,128)}) fusion(bf16[1024,2048]{1,0:T(8,128)(2,1)} %bitcast.1, bf16[2048,2560]{1,0:T(8,128)(2,1)} %param.7), kind=kOutput, calls=%fused_computation.22 | convolution fusion | flops 10740038656 | bytes 25169920 | tf_op jit(solution)/shard_map/dot_general | solution.py:8
  131.2 71.5 %pmax.7 = f32[1024]{0:T(1024)S(1)} all-reduce(f32[1024]{0:T(1024)S(1)} %get-tuple-element.11), channel_id=1, replica_groups=mesh['req'=8,'vocab'=32] {'vocab'}, use_global_device_ids=true, to_apply=%region_3.0 | all-reduce | flops 1024 | bytes 8192 | tf_op jit(solution)/shard_map/pmax | solution.py:55
  202.7 6.3 %fusion = (f32[1024]{0:T(1024)S(1)}, f32[1024]{0:T(1024)S(1)}) fusion(f32[1024,2560]{1,0:T(8,128)} %get-tuple-element.12, f32[1024]{0:T(1024)S(1)} %get-tuple-element.11), kind=kLoop, calls=%fused_computation.3 | loop fusion | flops 10483712 | bytes 10498048 | tf_op jit(solution)/shard_map/reduce_sum | solution.py:13
  209.0 17.0 %gather_fusion = f32[1024]{0:T(1024)S(1)} fusion(f32[1024,2560]{1,0:T(8,128)} %get-tuple-element.12, s32[1024]{0:T(1024)S(1)} %bitcast.9), kind=kCustom, calls=%fused_computation | custom fusion | bytes 16384 | tf_op jit(solution)/shard_map/jit(take_along_axis)/gather | solution.py:17
  226.1 138.0 %all-reduce = (f32[1024]{0:T(1024)S(1)}, f32[1024]{0:T(1024)S(1)}, f32[1024]{0:T(1024)S(1)}) all-reduce(f32[1024]{0:T(1024)S(1)} %select_select_fusion, f32[1024]{0:T(1024)S(1)} %get-tuple-element.8, f32[1024]{0:T(1024)S(1)} %get-tuple-element.7), channel_id=1, replica_groups=mesh['req'=8,'vocab'=32] {'vocab'}, use_global_device_ids=true, to_apply=%region_1.0 | all-reduce | flops 3072 | bytes 24576 | tf_op jit(solution)/shard_map/psum | solution.py:57
  364.1 0.6 compare_select_fusion.1
  (7 shorter events, 0.1 us)
Async XLA Ops:
  0.6 16.6 %copy-start = (s32[1024]{0:T(1024)S(1)}, s32[1024]{0:T(1024)}, u32[]{:S(2)}) copy-start(s32[1024]{0:T(1024)} %param.8) | copy-start | bytes 12292
  5.2 108.4 %all-to-all-start = ((bf16[32,32,2048]{2,1,0:T(8,128)(2,1)}), bf16[32,32,2048]{2,1,0:T(8,128)(2,1)}, u32[]{:S(2)}, u32[]{:S(2)}) async-start(bf16[32,32,2048]{2,1,0:T(8,128)(2,1)} %stack.2), calls=%async_computation | async-start | bytes 8388608 | tf_op jit(solution)/shard_map/all_to_all | solution.py:48
